TPU v7x, 32 devices: a whole 2x2x4 slice. The times are simulated.
32 devices in a mesh: seq: 16 (over z, y, x), head: 2 (over core).
Axes of the slice: x: 2, y: 2, z: 4, core: 2. Of those that a mesh axis runs over, the one named last changes fastest.
Arguments:
- queries: bfloat16 [2048, 16, 128], P('seq', 'head'), may hold values from -6 to 6
- key_vectors: bfloat16 [2048, 16, 128], P('seq', 'head'), may hold values from -16 to 16
- values: bfloat16 [2048, 16, 128], P('seq', 'head'), may hold values from -6 to 6
- out_gate: bfloat16 [2048, 16, 128], P('seq', 'head'), may hold values from -6 to 6
- inputs: bfloat16 [2048, 2048], P('seq', 'head'), may hold values from -6 to 6
- beta_weight: bfloat16 [16, 2048], P(None, 'head'), may hold values from -0.1875 to 0.1875
- log_decay: float32 [16, 2048], P('head', 'seq'), may hold values from -1 to 0
- initial_state: float32 [16, 128, 128], P('head'), may hold values from -6 to 6
Outputs:
- gated_out: bfloat16 [2048, 16, 128], P('seq', 'head')
- block_states: float32 [32, 16, 128, 128], P('seq', 'head')
All inputs are finite; a program needn't handle non-finite values.
Results may differ from a plain program's by a relative error of at most 0.0012.
Values sent between devices are 32-bit elements; how exact they have to be, the bound alone decides.
No kernel may reach another device: no remote copies, remote signals or barrier semaphores. Data moves between devices by JAX's collectives and lax.ppermute only.
A program may use at most 64 MiB of HBM per device.

v0:
```python
import jax
import jax.numpy as jnp
from jax import lax
from jax.sharding import PartitionSpec as P

BLOCK = 64
EPSILON = 1e-06


def entering(value, axis, join, neutral):
    count, mine = (lax.axis_size(axis), lax.axis_index(axis))
    pieces = jax.tree.map(lambda part: lax.all_gather(part, axis), value)
    so_far = jax.tree.map(
        lambda part, zero: jnp.full_like(part, 0) + jnp.asarray(zero, part.dtype), value, neutral
    )

    def step(position, so_far):
        longer = join(so_far, jax.tree.map(lambda part: part[position], pieces))
        return jax.tree.map(lambda new, old: jnp.where(position < mine, new, old), longer, so_far)

    return lax.fori_loop(0, count - 1, step, so_far)


def matmul(matrix, operand):
    return jnp.einsum("...ij,...jk->...ik", matrix, operand, precision=lax.Precision.HIGHEST)


def normalize(query_block, key_block, key_limit):
    query_float = query_block.astype(jnp.float32)
    key_float = key_block.astype(jnp.float32)
    queries_unit = (
        query_float
        / jnp.sqrt(jnp.sum(query_float * query_float, -1, keepdims=True) + EPSILON)
        * query_float.shape[-1] ** (-0.5)
    )
    keys_unit = key_float / jnp.maximum(
        jnp.sqrt(jnp.sum(key_float * key_float, -1, keepdims=True)), key_limit
    )
    return (queries_unit, keys_unit)


def block_parts(queries_unit, keys_unit, value_rows, beta_gate, decay_rows):
    length = decay_rows.shape[-1]
    feature = keys_unit.shape[-1]
    cumulative = jnp.cumsum(decay_rows, axis=-1)
    inside = jnp.tril(jnp.ones((length, length), jnp.float32))
    strict = jnp.tril(jnp.ones((length, length), jnp.float32), -1)
    spread = jnp.where(inside > 0, cumulative[..., :, None] - cumulative[..., None, :], 0.0)
    damping = jnp.exp(spread) * inside
    intersections = jnp.einsum(
        "...id,...jd->...ij", keys_unit, keys_unit, precision=lax.Precision.HIGHEST
    )
    system = (
        jnp.eye(length, dtype=jnp.float32)
        + beta_gate[..., :, None] * intersections * damping * strict
    )
    right_side = jnp.concatenate(
        [
            (beta_gate * jnp.exp(cumulative))[..., None] * keys_unit,
            beta_gate[..., None] * value_rows,
        ],
        axis=-1,
    )
    solved = lax.linalg.triangular_solve(
        system, right_side, left_side=True, lower=True, unit_diagonal=True
    )
    write_keys = solved[..., :feature]
    write_values = solved[..., feature:]
    final_sum = cumulative[..., -1:]
    carried = keys_unit * jnp.exp(final_sum - cumulative)[..., None]
    transition = jnp.exp(final_sum)[..., None] * jnp.eye(feature, dtype=jnp.float32) - jnp.einsum(
        "...ld,...le->...de", carried, write_keys, precision=lax.Precision.HIGHEST
    )
    offset = jnp.einsum(
        "...ld,...le->...de", carried, write_values, precision=lax.Precision.HIGHEST
    )
    reached = queries_unit * jnp.exp(cumulative)[..., None]
    scores = (
        jnp.einsum("...id,...jd->...ij", queries_unit, keys_unit, precision=lax.Precision.HIGHEST)
        * damping
    )
    return (write_keys, write_values, transition, offset, reached, scores)


def block_out(block_info, state_now):
    write_keys, write_values, transition, offset, reached, scores = block_info
    corrected = write_values - matmul(write_keys, state_now)
    return matmul(reached, state_now) + matmul(scores, corrected)


def gate_norm(raw_out, gate_rows):
    inverse_rms = 1.0 / jnp.sqrt(jnp.mean(raw_out * raw_out, -1, keepdims=True) + EPSILON)
    return (raw_out * inverse_rms * jax.nn.silu(gate_rows.astype(jnp.float32))).astype(jnp.bfloat16)


def combine(earlier, latter):
    return (matmul(latter[0], earlier[0]), matmul(latter[0], earlier[1]) + latter[1])


def advance(queries_unit, keys_unit, value_rows, beta_gate, decay_rows, start_state):
    block_info = block_parts(queries_unit, keys_unit, value_rows, beta_gate, decay_rows)
    transition = jnp.moveaxis(block_info[2], 1, 0)
    offset = jnp.moveaxis(block_info[3], 1, 0)
    head_count = transition.shape[1]
    feature = transition.shape[2]
    identity_map = jnp.broadcast_to(
        jnp.eye(feature, dtype=jnp.float32), (head_count, feature, feature)
    )
    zero_state = jnp.zeros((head_count, feature, value_rows.shape[-1]), jnp.float32)

    def compose(carried_map, block_map):
        return (
            (
                matmul(block_map[0], carried_map[0]),
                matmul(block_map[0], carried_map[1]) + block_map[1],
            ),
            carried_map,
        )

    (device_map, device_offset), prefixes = lax.scan(
        compose, (identity_map, zero_state), (transition, offset)
    )
    before_map, before_offset = entering(
        (device_map, device_offset), "seq", combine, (identity_map, zero_state)
    )
    entry_state = matmul(before_map, start_state) + before_offset
    starts = matmul(prefixes[0], entry_state[None]) + prefixes[1]
    raw_out = block_out(block_info, jnp.moveaxis(starts, 0, 1))
    return (raw_out, starts)


def on_device(
    queries, key_vectors, values, out_gate, inputs, beta_weight, log_decay, initial_state
):
    token_count, head_count, feature = queries.shape
    blocks = token_count // BLOCK
    logits = lax.psum_scatter(
        lax.dot_general(
            beta_weight, inputs, (((1,), (1,)), ((), ())), preferred_element_type=jnp.float32
        ),
        "head",
        scatter_dimension=0,
        tiled=True,
    )
    beta_gate = jax.nn.sigmoid(logits)
    key_float = key_vectors.astype(jnp.float32)
    key_total = lax.psum(jnp.sum(key_float * key_float, axis=(0, 2)), "seq")
    key_limit = jnp.sqrt(key_total / (token_count * lax.axis_size("seq")) + EPSILON)
    queries_unit, keys_unit = normalize(queries, key_vectors, key_limit[:, None])

    def arrange(tensor):
        return tensor.reshape(blocks, BLOCK, head_count, -1).transpose(2, 0, 1, 3)

    query_blocks = arrange(queries_unit)
    key_blocks = arrange(keys_unit)
    value_blocks = arrange(values.astype(jnp.float32))
    beta_blocks = beta_gate.reshape(head_count, blocks, BLOCK)
    decay_blocks = log_decay.reshape(head_count, blocks, BLOCK)
    raw_out, starts = advance(
        query_blocks, key_blocks, value_blocks, beta_blocks, decay_blocks, initial_state
    )
    gated_out = gate_norm(
        raw_out.transpose(1, 2, 0, 3).reshape(token_count, head_count, feature), out_gate
    )
    return (gated_out, starts)


def solution(mesh):
    return jax.shard_map(
        on_device,
        mesh=mesh,
        in_specs=(
            P("seq", "head", None),
            P("seq", "head", None),
            P("seq", "head", None),
            P("seq", "head", None),
            P("seq", "head"),
            P(None, "head"),
            P("head", "seq"),
            P("head", None, None),
        ),
        out_specs=(P("seq", "head", None), P("seq", "head", None, None)),
        check_vma=False,
    )
```

profile of v0, /device:TPU:0, one launch (start us, length us, event | category | flops | bytes accessed | tf_op | source)
XLA Modules:
  0.0 458.2 jit_solution(17087418341831936964)
XLA Ops:
  10.1 43.5 %psum.7 = f32[8]{0:T(128)S(1)} all-reduce(f32[8]{0:T(128)S(1)} %get-tuple-element.239), channel_id=1, replica_groups=mesh['seq'=16,'head'=2] {'seq'}, use_global_device_ids=true, to_apply=%region_4.0 | all-reduce | flops 8 | bytes 64 | tf_op jit(solution)/shard_map/psum | solution.py:147
  55.0 1.3 fusion.68
  56.3 2.5 all-reduce
  61.8 78.6 %custom-call.3 = f32[8,2,1,64,64]{3,4,2,1,0:T(8,128)S(1)} custom-call(f32[8,2,1,64,64]{4,3,2,1,0:T(8,128)S(1)} %fusion.30), custom_call_target="InvertDiagBlocksLowerTriangular" | custom-call | tf_op jit(solution)/shard_map/triangular_solve | solution.py:64
  143.0 3.0 convolution_bitcast_fusion
  146.0 2.0 fusion.22
  148.1 12.5 %while.33 = (s32[]{:T(128)}, f32[8,128,128]{2,1,0:T(8,128)S(1)}, f32[8,128,128]{2,1,0:T(8,128)}, f32[2,8,128,128]{3,2,0,1:T(8,128)}, f32[2,8,128,128]{2,3,0,1:T(...) while((s32[]{:T(128)}, f32[8,128,128]{2,1,0:T(8,128)S(1)}, ...), condition=%wide.region_7.8_spmd.clone, body=%wide.region_6.7_spmd.clone.sunk | while | flops 403046400 | bytes 9963628 | solution.py:120
  149.2 2.5 convolution_add_fusion.5
  155.4 2.5 convolution_add_fusion.5
  162.7 2.8 convolution_multiply_fusion
  165.5 104.3 %all-gather.5.cloned.1.call-done = f32[128,128,128]{2,1,0:T(8,128)} async-done(((f32[8,128,128]{2,1,0:T(8,128)}), f32[128,128,128]{2,1,0:T(8,128)}) %all-gather.5.cloned.1.call-update) | async-done | bytes 8388624 | tf_op jit(solution)/shard_map/all_gather | solution.py:12
  269.8 113.3 %all-gather.7.cloned.1.call-done = f32[128,128,128]{2,1,0:T(8,128)} async-done(((f32[8,128,128]{2,1,0:T(8,128)}), f32[128,128,128]{2,1,0:T(8,128)}) %all-gather.7.cloned.1.call-update) | async-done | bytes 8388624 | tf_op jit(solution)/shard_map/all_gather | solution.py:12
  383.1 55.4 %while.34 = (s32[]{:T(128)}, f32[8,128,128]{2,1,0:T(8,128)S(1)}, f32[8,128,128]{2,1,0:T(8,128)S(1)}, s32[]{:T(128)}, f32[16,8,128,128]{3,2,1,0:T(8,128)}, /*index=5*/f32[16,8,128,128]{3,2,1,0:T(8,128)}, s32[]{:T(128)}, s32[]{:T(128)}) while((s32[]{:T(128)}, f32[8,128,128]{2,1,0:T(8,128)S(1)}, f32[8,128,128]{2,1,0:T(8,128)S(1)}, ...), condition=%wide.region_9.10_spmd.clone, body=%wide.region_8.9_spmd.clone.sunk | while | flops 403308544 | bytes 6818920 | solution.py:21
  383.2 1.9 fusion.102
  385.2 1.7 convolution_select_fusion.2
  386.9 1.9 fusion.102
  388.9 1.7 convolution_select_fusion.2
  390.6 1.9 fusion.102
  392.5 1.7 convolution_select_fusion.2
  394.3 1.9 fusion.102
  396.2 1.7 convolution_select_fusion.2
  398.0 1.9 fusion.102
  399.9 1.7 convolution_select_fusion.2
  401.7 1.9 fusion.102
  403.6 1.7 convolution_select_fusion.2
  405.4 1.9 fusion.102
  407.3 1.7 convolution_select_fusion.2
  409.1 1.9 fusion.102
  411.0 1.7 convolution_select_fusion.2
  412.8 1.9 fusion.102
  414.7 1.7 convolution_select_fusion.2
  416.4 1.9 fusion.102
  418.4 1.7 convolution_select_fusion.2
  420.1 1.9 fusion.102
  422.1 1.7 convolution_select_fusion.2
  423.8 1.9 fusion.102
  425.7 1.7 convolution_select_fusion.2
  427.5 1.9 fusion.102
  429.4 1.7 convolution_select_fusion.2
  431.2 1.9 fusion.102
  433.1 1.7 convolution_select_fusion.2
  434.9 1.9 fusion.102
  436.8 1.7 convolution_select_fusion.2
  439.2 2.6 fusion.23
  441.8 2.9 convolution_subtract_fusion
  444.7 1.3 copy.94
  446.0 1.8 fusion.69
  447.9 2.2 fusion.45
  (103 shorter events, 21.5 us)
Async XLA Ops:
  7.2 431.4 %copy-start = (f32[8,128,128]{2,1,0:T(8,128)S(1)}, f32[8,128,128]{2,1,0:T(8,128)}, u32[]{:S(2)}) copy-start(f32[8,128,128]{2,1,0:T(8,128)} %param.19) | copy-start | bytes 1572868
  7.2 262.6 %all-gather.5.cloned.1.call-start = ((), (), s32[]{:S(2)}) async-start(), calls=%async_computation | async-start | bytes 8912896 | tf_op jit(solution)/shard_map/all_gather | solution.py:12
  55.0 91.0 %copy-start.2 = (f32[128,8,128]{2,0,1:T(8,128)}, f32[128,8,128]{2,0,1:T(8,128)S(1)}, u32[]{:S(2)}) copy-start(f32[128,8,128]{2,0,1:T(8,128)S(1)} %copy.77) | copy-start | bytes 1572868
  143.0 5.0 %copy-start.3 = (f32[8,2,64,256]{3,2,1,0:T(8,128)}, f32[8,2,64,256]{3,2,1,0:T(8,128)S(1)}, u32[]{:S(2)}) copy-start(f32[8,2,64,256]{3,2,1,0:T(8,128)S(1)} %fusion.31) | copy-start | bytes 3145732
  148.1 14.1 %copy-start.5 = (bf16[128,8,128]{2,1,0:T(8,128)(2,1)S(1)}, bf16[128,8,128]{2,1,0:T(8,128)(2,1)}, u32[]{:S(2)}) copy-start(bf16[128,8,128]{2,1,0:T(8,128)(2,1)} %param.12) | copy-start | bytes 786436
  160.6 0.8 copy-start.1
  161.4 221.7 %all-gather.7.cloned.1.call-start = ((), (), s32[]{:S(2)}) async-start(), calls=%async_computation.1 | async-start | bytes 8912896 | tf_op jit(solution)/shard_map/all_gather | solution.py:12
  383.1 58.7 %copy-start.4 = (f32[8,2,64,256]{3,2,1,0:T(8,128)S(1)}, f32[8,2,64,256]{3,2,1,0:T(8,128)}, u32[]{:S(2)}) copy-start(f32[8,2,64,256]{3,2,1,0:T(8,128)} %copy-done.3) | copy-start | bytes 3145732
  438.5 11.7 %copy-start.6 = (bf16[128,8,128]{2,1,0:T(8,128)(2,1)S(1)}, bf16[128,8,128]{2,1,0:T(8,128)(2,1)}, u32[]{:S(2)}) copy-start(bf16[128,8,128]{2,1,0:T(8,128)(2,1)} %param.15) | copy-start | bytes 786436
Sparse Core Ops, SparseCore 0:
  161.5 108.2 all-gather.4
  272.6 110.4 all-gather.6
where the time goes:
time: 460 us; the launch traced here: 458 us
  waiting for transfers between devices  218 us (47%)
  other arithmetic  83.8 us (18%)
  matrix products  81.3 us (18%)
  blocking collectives  46 us (10%)
  between operations  15 us (3%)
  local copies, waits for them, and re-layouts  12.8 us (3%)
    all_gather x2, waiting for transfers between devices, entering(): pieces = jax.tree.map(lambda part: lax.all_gather(part, axis), value)  218 us
    another operation x4, other arithmetic, block_parts(): lax.linalg.triangular_solve(system, right_side, left_side=True, lower=Tru...  78.7 us
    dot_general x39, matrix products, matmul(): jnp.einsum('...ij,...jk->...ik', matrix, operand, precision=lax.Precision...  70 us
    psum x1, blocking collectives, on_device(): key_total = lax.psum(jnp.sum(key_float * key_float, axis=(0, 2)), 'seq')  43.5 us
  transfers between devices with their start and end apart: 2, of which 2 were waited for; matrix products, arithmetic and copies ran while one was open for 1% of the time, Pallas kernels for 0%

commit v1 on v0

--- a/solution.py
+++ b/solution.py
@@ -144,7 +144,9 @@
     )
     beta_gate = jax.nn.sigmoid(logits)
     key_float = key_vectors.astype(jnp.float32)
-    key_total = lax.psum(jnp.sum(key_float * key_float, axis=(0, 2)), "seq")
+    own = jnp.sum(key_float * key_float, axis=(0, 2))
+    parts = lax.all_gather(own, "seq", axis=0, tiled=False)
+    key_total = parts.sum(axis=0)
     key_limit = jnp.sqrt(key_total / (token_count * lax.axis_size("seq")) + EPSILON)
     queries_unit, keys_unit = normalize(queries, key_vectors, key_limit[:, None])
 

time: 460 us -> 462 us (level)
    psum x1 -> x0, blocking collectives: 43.5 us -> none  [on_device(): key_total = lax.psum(jnp.sum(key_float * key_float, axis=(0, 2)), 'seq')]
    unnamed x1 -> x2, blocking collectives: 2.49 us -> 46 us
where the time goes in v1:
time: 462 us; the launch traced here: 460 us
  waiting for transfers between devices  218 us (47%)
  other arithmetic  83.8 us (18%)
  matrix products  81.3 us (18%)
  blocking collectives  46 us (10%)
  between operations  15.7 us (3%)
  local copies, waits for them, and re-layouts  14.4 us (3%)
    all_gather x2, waiting for transfers between devices, entering(): pieces = jax.tree.map(lambda part: lax.all_gather(part, axis), value)  218 us
    another operation x4, other arithmetic, block_parts(): lax.linalg.triangular_solve(system, right_side, left_side=True, lower=Tru...  78.7 us
    dot_general x39, matrix products, matmul(): jnp.einsum('...ij,...jk->...ik', matrix, operand, precision=lax.Precision...  70 us
    unnamed x2, blocking collectives  46 us
  transfers between devices with their start and end apart: 2, of which 2 were waited for; matrix products, arithmetic and copies ran while one was open for 1% of the time, Pallas kernels for 0%

profile of v1, /device:TPU:0, one launch (start us, length us, event | category | flops | bytes accessed | tf_op | source)
XLA Modules:
  0.0 460.5 jit_solution(11357983003086680550)
XLA Ops:
  12.3 43.5 %all-reduce = f32[128]{0:T(128)S(1)} all-reduce(f32[128]{0:T(128)S(1)} %dynamic-update-slice), channel_id=2, replica_groups=mesh['seq'=16,'head'=2] {'seq'}, use_global_device_ids=true, to_apply=%add | all-reduce | flops 128 | bytes 1024
  57.2 1.3 fusion.68
  58.6 2.5 all-reduce.1
  64.0 78.6 %custom-call.3 = f32[8,2,1,64,64]{3,4,2,1,0:T(8,128)S(1)} custom-call(f32[8,2,1,64,64]{4,3,2,1,0:T(8,128)S(1)} %fusion.30), custom_call_target="InvertDiagBlocksLowerTriangular" | custom-call | tf_op jit(solution)/shard_map/triangular_solve | solution.py:64
  145.3 3.0 convolution_bitcast_fusion
  148.3 2.0 fusion.22
  150.4 12.5 %while.33 = (s32[]{:T(128)}, f32[8,128,128]{2,1,0:T(8,128)S(1)}, f32[8,128,128]{2,1,0:T(8,128)}, f32[2,8,128,128]{3,2,0,1:T(8,128)}, f32[2,8,128,128]{2,3,0,1:T(...) while((s32[]{:T(128)}, f32[8,128,128]{2,1,0:T(8,128)S(1)}, ...), condition=%wide.region_7.8_spmd.clone, body=%wide.region_6.7_spmd.clone.sunk | while | flops 403046400 | bytes 9963628 | solution.py:120
  151.5 2.5 convolution_add_fusion.5
  157.7 2.5 convolution_add_fusion.5
  164.9 2.8 convolution_multiply_fusion
  167.8 104.3 %all-gather.6.cloned.1.call-done = f32[128,128,128]{2,1,0:T(8,128)} async-done(((f32[8,128,128]{2,1,0:T(8,128)}), f32[128,128,128]{2,1,0:T(8,128)}) %all-gather.6.cloned.1.call-update) | async-done | bytes 8388624 | tf_op jit(solution)/shard_map/all_gather | solution.py:12
  272.0 113.3 %all-gather.8.cloned.1.call-done = f32[128,128,128]{2,1,0:T(8,128)} async-done(((f32[8,128,128]{2,1,0:T(8,128)}), f32[128,128,128]{2,1,0:T(8,128)}) %all-gather.8.cloned.1.call-update) | async-done | bytes 8388624 | tf_op jit(solution)/shard_map/all_gather | solution.py:12
  385.4 55.4 %while.34 = (s32[]{:T(128)}, f32[8,128,128]{2,1,0:T(8,128)S(1)}, f32[8,128,128]{2,1,0:T(8,128)S(1)}, s32[]{:T(128)}, f32[16,8,128,128]{3,2,1,0:T(8,128)}, /*index=5*/f32[16,8,128,128]{3,2,1,0:T(8,128)}, s32[]{:T(128)}, s32[]{:T(128)}) while((s32[]{:T(128)}, f32[8,128,128]{2,1,0:T(8,128)S(1)}, f32[8,128,128]{2,1,0:T(8,128)S(1)}, ...), condition=%wide.region_9.10_spmd.clone, body=%wide.region_8.9_spmd.clone.sunk | while | flops 403308544 | bytes 6818920 | solution.py:21
  385.4 1.9 fusion.102
  387.4 1.7 convolution_select_fusion.2
  389.2 1.9 fusion.102
  391.1 1.7 convolution_select_fusion.2
  392.9 1.9 fusion.102
  394.8 1.7 convolution_select_fusion.2
  396.6 1.9 fusion.102
  398.5 1.7 convolution_select_fusion.2
  400.3 1.9 fusion.102
  402.2 1.7 convolution_select_fusion.2
  403.9 1.9 fusion.102
  405.9 1.7 convolution_select_fusion.2
  407.6 1.9 fusion.102
  409.6 1.7 convolution_select_fusion.2
  411.3 1.9 fusion.102
  413.2 1.7 convolution_select_fusion.2
  415.0 1.9 fusion.102
  416.9 1.7 convolution_select_fusion.2
  418.7 1.9 fusion.102
  420.6 1.7 convolution_select_fusion.2
  422.4 1.9 fusion.102
  424.3 1.7 convolution_select_fusion.2
  426.1 1.9 fusion.102
  428.0 1.7 convolution_select_fusion.2
  429.8 1.9 fusion.102
  431.7 1.7 convolution_select_fusion.2
  433.5 1.9 fusion.102
  435.4 1.7 convolution_select_fusion.2
  437.1 1.9 fusion.102
  439.1 1.7 convolution_select_fusion.2
  441.5 2.6 fusion.23
  444.1 2.9 convolution_subtract_fusion
  447.0 1.3 copy.94
  448.3 1.8 fusion.69
  450.1 2.2 fusion.45
  (108 shorter events, 23.1 us)
Async XLA Ops:
  7.2 433.6 %copy-start = (f32[8,128,128]{2,1,0:T(8,128)S(1)}, f32[8,128,128]{2,1,0:T(8,128)}, u32[]{:S(2)}) copy-start(f32[8,128,128]{2,1,0:T(8,128)} %param.19) | copy-start | bytes 1572868
  7.2 264.9 %all-gather.6.cloned.1.call-start = ((), (), s32[]{:S(2)}) async-start(), calls=%async_computation | async-start | bytes 8912896 | tf_op jit(solution)/shard_map/all_gather | solution.py:12
  57.2 91.0 %copy-start.2 = (f32[128,8,128]{2,0,1:T(8,128)}, f32[128,8,128]{2,0,1:T(8,128)S(1)}, u32[]{:S(2)}) copy-start(f32[128,8,128]{2,0,1:T(8,128)S(1)} %copy.77) | copy-start | bytes 1572868
  145.3 5.0 %copy-start.3 = (f32[8,2,64,256]{3,2,1,0:T(8,128)}, f32[8,2,64,256]{3,2,1,0:T(8,128)S(1)}, u32[]{:S(2)}) copy-start(f32[8,2,64,256]{3,2,1,0:T(8,128)S(1)} %fusion.31) | copy-start | bytes 3145732
  150.3 14.1 %copy-start.5 = (bf16[128,8,128]{2,1,0:T(8,128)(2,1)S(1)}, bf16[128,8,128]{2,1,0:T(8,128)(2,1)}, u32[]{:S(2)}) copy-start(bf16[128,8,128]{2,1,0:T(8,128)(2,1)} %param.12) | copy-start | bytes 786436
  162.8 0.8 copy-start.1
  163.7 221.7 %all-gather.8.cloned.1.call-start = ((), (), s32[]{:S(2)}) async-start(), calls=%async_computation.1 | async-start | bytes 8912896 | tf_op jit(solution)/shard_map/all_gather | solution.py:12
  385.4 58.7 %copy-start.4 = (f32[8,2,64,256]{3,2,1,0:T(8,128)S(1)}, f32[8,2,64,256]{3,2,1,0:T(8,128)}, u32[]{:S(2)}) copy-start(f32[8,2,64,256]{3,2,1,0:T(8,128)} %copy-done.3) | copy-start | bytes 3145732
  440.8 11.7 %copy-start.6 = (bf16[128,8,128]{2,1,0:T(8,128)(2,1)S(1)}, bf16[128,8,128]{2,1,0:T(8,128)(2,1)}, u32[]{:S(2)}) copy-start(bf16[128,8,128]{2,1,0:T(8,128)(2,1)} %param.15) | copy-start | bytes 786436
Sparse Core Ops, SparseCore 0:
  163.8 108.2 all-gather.5
  274.8 110.4 all-gather.7
